TPU v7x, 32 devices: a whole 2x2x4 slice. The times are simulated.
32 devices in a mesh: ctx: 16 (over z, x, core), tp: 2 (over y).
Axes of the slice: x: 2, y: 2, z: 4, core: 2. Of those that a mesh axis runs over, the one named last changes fastest.
Arguments:
- queries: bfloat16 [16384, 4096], P('ctx', 'tp'), may hold values from -96 to 96
- rotated_key_rows: bfloat16 [16384, 2048], P('ctx', 'tp'), may hold values from -5 to 5
- value_head_rows: bfloat16 [16384, 2048], P('ctx', 'tp'), may hold values from -5 to 5
- w_out: bfloat16 [16, 256, 3840], P('tp', 'ctx'), may hold values from -0.09375 to 0.09375
- post_gain: float32 [3840], replicated, may hold values from 0.25 to 1.75
- doc_lengths: int32 [16], replicated, may hold values from 1 to 4096, 16384 in all
Outputs:
- normed_out: bfloat16 [16384, 3840], P(('ctx', 'tp'))
All inputs are finite; a program needn't handle non-finite values.
Results may differ from a plain program's by a relative error of at most 0.0085.
Values may be sent and summed in bfloat16 or wider, within the bound.
No kernel may reach another device: no remote copies, remote signals or barrier semaphores. Data moves between devices by JAX's collectives and lax.ppermute only.
A program may use at most 192 MiB of HBM per device.

v0:
```python
import jax
import jax.numpy as jnp
from jax import lax
from jax.sharding import PartitionSpec as P

HEAD_SIZE = 256
ATTEND_WINDOW = 1024


def shifted(shard, axis, by):
    devices = lax.axis_size(axis)
    pairs = [(i, i + by) for i in range(devices) if 0 <= i + by < devices]
    return lax.ppermute(shard, axis, pairs)


def post_norm(summed, post_gain):
    mean_sq = jnp.mean(summed * summed, axis=-1, keepdims=True)
    return (summed * lax.rsqrt(mean_sq + 1e-06) * post_gain).astype(jnp.bfloat16)


def score_part(query_block, key_portion, kv_heads, scaling):
    key_block = key_portion.reshape(key_portion.shape[0], kv_heads, HEAD_SIZE)
    return (
        jnp.einsum("qhgd,khd->hgqk", query_block, key_block, preferred_element_type=jnp.float32)
        * scaling
    )


def on_device(queries, rotated_key_rows, value_head_rows, w_out, post_gain, doc_lengths):
    tok_local = queries.shape[0]
    kv_heads = rotated_key_rows.shape[1] // HEAD_SIZE
    heads_local = queries.shape[1] // HEAD_SIZE
    head_groups = heads_local // kv_heads
    scaling = HEAD_SIZE ** (-0.5)
    query_block_size = min(512, tok_local)
    key_block_size = ATTEND_WINDOW + query_block_size
    block_total = tok_local // query_block_size
    query_blocks = [
        queries[b * query_block_size : (b + 1) * query_block_size].reshape(
            query_block_size, kv_heads, head_groups, HEAD_SIZE
        )
        for b in range(block_total)
    ]
    key_parts = []
    val_parts = []
    arrived = shifted((rotated_key_rows, value_head_rows), "ctx", 1)
    key_parts.insert(0, arrived[0])
    val_parts.insert(0, arrived[1])
    halo_keys = key_parts[0]
    all_vals = jnp.concatenate(val_parts + [value_head_rows], axis=0)
    base = lax.axis_index("ctx") * tok_local
    qpos_all = base + jnp.arange(tok_local, dtype=jnp.int32)
    kpos_all = base - ATTEND_WINDOW + jnp.arange(ATTEND_WINDOW + tok_local, dtype=jnp.int32)
    doc_ends = jnp.cumsum(doc_lengths)
    qdoc_all = jnp.sum((doc_ends[None, :] <= qpos_all[:, None]).astype(jnp.int32), axis=1)
    kdoc_all = jnp.sum((doc_ends[None, :] <= kpos_all[:, None]).astype(jnp.int32), axis=1)
    outputs = []
    for block_id in range(block_total):
        lower = block_id * query_block_size
        local_lo = max(lower, ATTEND_WINDOW) - ATTEND_WINDOW
        local_hi = lower + key_block_size - ATTEND_WINDOW
        local_scores = score_part(
            query_blocks[block_id], rotated_key_rows[local_lo:local_hi], kv_heads, scaling
        )
        halo_scores = score_part(
            query_blocks[block_id], halo_keys[lower:ATTEND_WINDOW], kv_heads, scaling
        )
        scores = jnp.concatenate([halo_scores, local_scores], axis=-1)
        value_block = all_vals[lower : lower + key_block_size].reshape(
            key_block_size, kv_heads, HEAD_SIZE
        )
        qpos = qpos_all[lower : lower + query_block_size]
        kpos = kpos_all[lower : lower + key_block_size]
        qdoc = qdoc_all[lower : lower + query_block_size]
        kdoc = kdoc_all[lower : lower + key_block_size]
        allowed = (
            (kpos[None, :] >= 0)
            & (kpos[None, :] <= qpos[:, None])
            & (qpos[:, None] - kpos[None, :] < ATTEND_WINDOW)
            & (kdoc[None, :] == qdoc[:, None])
        )
        scores = jnp.where(allowed[None, None], scores, -jnp.inf)
        top = jnp.max(scores, axis=-1, keepdims=True)
        expo = jnp.exp(scores - top)
        weights = (expo / jnp.sum(expo, axis=-1, keepdims=True)).astype(jnp.bfloat16)
        result = jnp.einsum(
            "hgqk,khd->qhgd", weights, value_block, preferred_element_type=jnp.float32
        )
        outputs.append(
            result.reshape(query_block_size, heads_local * HEAD_SIZE).astype(jnp.bfloat16)
        )
    attn = jnp.concatenate(outputs, axis=0).reshape(tok_local, heads_local, HEAD_SIZE)
    partial_value = jnp.einsum(
        "thn,hnd->td",
        attn,
        lax.all_gather(w_out, "ctx", axis=1, tiled=True),
        preferred_element_type=jnp.float32,
    )
    mine = lax.psum_scatter(
        partial_value.astype(jnp.bfloat16), "tp", scatter_dimension=0, tiled=True
    ).astype(jnp.float32)
    return post_norm(mine, post_gain)


def solution(mesh):
    placed = (P("ctx", "tp"), P("ctx", "tp"), P("ctx", "tp"), P("tp", "ctx", None), P(), P())
    return jax.shard_map(
        on_device, mesh=mesh, in_specs=placed, out_specs=P(("ctx", "tp"), None), check_vma=False
    )
```

profile of v0, /device:TPU:0, one launch (start us, length us, event | category | flops | bytes accessed | tf_op | source)
XLA Modules:
  0.0 379.6 jit_solution(13983909736662050847)
XLA Ops:
  6.5 0.7 all-gather.2.cloned.1.call-update
  7.3 4.0 %copy.36 = bf16[1024,1024]{0,1:T(8,128)(2,1)} copy(bf16[1024,1024]{1,0:T(8,128)(2,1)} %param.7) | data formatting | bytes 4194304 | tf_op args[1]
  11.3 3.8 %collective-permute-start.1 = (bf16[1024,1024]{0,1:T(8,128)(2,1)}, bf16[1024,1024]{0,1:T(8,128)(2,1)}, u32[]{:S(2)}, u32[]{:S(2)}) collective-permute-start(bf16[1024,1024]{0,1:T(8,128)(2,1)} %copy.36), channel_id=1, source_target_pairs={{0,2},{2,4},{4,6},{6,8},{8,10},{10,12},{12,14},{14,16},{16,18},{18... | collective-permute-start | bytes 6291464 | tf_op jit(solution)/shard_map/ppermute | solution.py:13
  15.1 4.5 %collective-permute-start = (bf16[1024,1024]{1,0:T(8,128)(2,1)}, bf16[1024,1024]{1,0:T(8,128)(2,1)}, u32[]{:S(2)}, u32[]{:S(2)}) collective-permute-start(bf16[1024,1024]{1,0:T(8,128)(2,1)} %param.8), channel_id=1, source_target_pairs={{0,2},{2,4},{4,6},{6,8},{8,10},{10,12},{12,14},{14,16},{16,18},{18... | collective-permute-start | bytes 6291464 | tf_op jit(solution)/shard_map/ppermute | solution.py:13
  19.6 1.4 slice.59
  21.0 2.8 reshape.281
  24.1 4.0 %fusion.26 = (bf16[512,2048]{1,0:T(8,128)(2,1)S(1)}, bf16[512,2048]{1,0:T(8,128)(2,1)}) fusion(bf16[1024,2048]{1,0:T(8,128)(2,1)} %param.6), kind=kLoop, calls=%fused_computation.50 | loop fusion | bytes 8388608 | tf_op jit(solution)/shard_map/slice | solution.py:39
  28.1 2.5 copy.73
  30.6 2.9 copy.74
  33.8 2.6 fusion.17
  36.4 2.6 fusion.19
  38.9 6.4 %multiply_bitcast_fusion.3 = f32[4,2,512,512]{2,3,1,0:T(8,128)} fusion(bf16[512,4,256,1]{0,2,3,1:T(8,128)(2,1)S(1)} %bitcast.60, bf16[512,4,2,256]{0,3,2,1:T(8,128)(2,1)} %bitcast.57), kind=kOutput, calls=%fused_computation.22 | convolution fusion | flops 1075838976 | bytes 11534336 | tf_op jit(solution)/shard_map/qhgd,khd->hgqk/dot_general | solution.py:24
  45.3 8.0 %multiply_bitcast_fusion = f32[4,2,512,1024]{2,3,1,0:T(8,128)} fusion(bf16[512,4,2,256]{0,3,2,1:T(8,128)(2,1)S(1)} %bitcast.55, bf16[1024,4,256,1]{2,1,0,3:T(4,128)(2,1)S(1)} %bitcast.59), kind=kOutput, calls=%fused_computation.10 | convolution fusion | flops 2151677952 | bytes 20971520 | tf_op jit(solution)/shard_map/qhgd,khd->hgqk/dot_general | solution.py:24
  53.4 1.9 constant_dynamic-update-slice_fusion.1
  55.3 0.3 copy-done.4
  55.8 3.5 fusion.27
  59.3 4.7 %copy.34 = bf16[1536,1024]{0,1:T(8,128)(2,1)} copy(bf16[1536,1024]{1,0:T(8,128)(2,1)} %get-tuple-element.7) | data formatting | bytes 6291456 | tf_op jit(solution)/shard_map/slice | solution.py:69
  63.9 4.7 %multiply_bitcast_fusion.1 = f32[4,2,512,1024]{2,3,1,0:T(8,128)S(1)} fusion(bf16[1024,4,256,1]{0,2,3,1:T(8,128)(2,1)} %bitcast.28, bf16[512,4,2,256]{0,3,2,1:T(8,128)(2,1)} %bitcast.58), kind=kOutput, calls=%fused_computation.11 | convolution fusion | flops 2151677952 | bytes 20971520 | tf_op jit(solution)/shard_map/qhgd,khd->hgqk/dot_general | solution.py:24
  68.6 14.9 %fusion.33 = (f32[4,2,512]{2,1,0:T(2,128)S(1)}, f32[4,2,512,1536]{2,3,1,0:T(8,128)}) fusion(f32[4,2,512,512]{2,3,1,0:T(8,128)} %multiply_bitcast_fusion.3, f32[4,2,512,1024]{2,3,1,0:T(8,128)S(1)} %multiply_bitcast_fusion.1, pred[512,1536]{0,1:T(8,128)(4,1)S(1)} %copy-done.6), kind=kOutput, calls=%fused_computation.57 | output fusion | flops 25167360 | bytes 51134464 | tf_op jit(solution)/shard_map/sub | solution.py:84
  83.5 14.1 %fusion.22 = bf16[4,256,2,512]{3,1,2,0:T(8,128)(2,1)} fusion(bf16[1536,4,256,1]{0,2,3,1:T(8,128)(2,1)} %bitcast.62, f32[4,2,512,1536]{2,3,1,0:T(8,128)} %get-tuple-element.22, f32[4,2,512]{2,1,0:T(2,128)S(1)} %get-tuple-element.21), kind=kOutput, calls=%fused_computation.37 | convolution fusion | flops 3234856960 | bytes 30425088 | tf_op jit(solution)/shard_map/hgqk,khd->qhgd/dot_general | solution.py:86
  97.6 3.9 %copy.51 = bf16[512,8,256]{2,0,1:T(8,128)(2,1)} copy(bf16[512,8,256]{0,2,1:T(8,128)(2,1)} %bitcast.64) | data formatting | bytes 4194304 | tf_op jit(solution)/shard_map/convert_element_type | solution.py:90
  101.6 4.6 %copy.44 = bf16[1536,1024]{0,1:T(8,128)(2,1)} copy(bf16[1536,1024]{1,0:T(8,128)(2,1)} %get-tuple-element.8) | data formatting | bytes 6291456 | tf_op jit(solution)/shard_map/slice | solution.py:69
  106.2 1.3 slice.63
  107.5 4.6 %multiply_bitcast_fusion.2 = f32[4,2,512,512]{2,3,1,0:T(8,128)} fusion(bf16[512,4,256,1]{0,2,3,1:T(8,128)(2,1)S(1)} %bitcast.61, bf16[512,4,2,256]{0,3,2,1:T(8,128)(2,1)S(1)} %bitcast.56), kind=kOutput, calls=%fused_computation.21 | convolution fusion | flops 1075838976 | bytes 11534336 | tf_op jit(solution)/shard_map/qhgd,khd->hgqk/dot_general | solution.py:24
  112.1 16.7 %fusion.32 = (f32[4,2,512]{2,1,0:T(2,128)S(1)}, f32[4,2,512,1536]{2,3,1,0:T(8,128)}) fusion(f32[4,2,512,1024]{2,3,1,0:T(8,128)} %multiply_bitcast_fusion, f32[4,2,512,512]{2,3,1,0:T(8,128)} %multiply_bitcast_fusion.2, pred[512,1536]{0,1:T(8,128)(4,1)} %fusion.19), kind=kOutput, calls=%fused_computation.56 | output fusion | flops 25167360 | bytes 51134464 | tf_op jit(solution)/shard_map/sub | solution.py:84
  128.8 13.1 %fusion.21 = bf16[4,256,2,512]{3,1,2,0:T(8,128)(2,1)} fusion(bf16[1536,4,256,1]{0,2,3,1:T(8,128)(2,1)S(1)} %bitcast.63, f32[4,2,512,1536]{2,3,1,0:T(8,128)} %get-tuple-element.20, f32[4,2,512]{2,1,0:T(2,128)S(1)} %get-tuple-element.19), kind=kOutput, calls=%fused_computation.36 | convolution fusion | flops 3234856960 | bytes 30425088 | tf_op jit(solution)/shard_map/hgqk,khd->qhgd/dot_general | solution.py:86
  141.9 4.1 %copy.52 = bf16[512,8,256]{2,0,1:T(8,128)(2,1)} copy(bf16[512,8,256]{0,2,1:T(8,128)(2,1)} %bitcast.65) | data formatting | bytes 4194304 | tf_op jit(solution)/shard_map/convert_element_type | solution.py:90
  145.9 15.4 %all-gather.2.cloned.1.call-done = bf16[8,256,3840]{2,1,0:T(8,128)(2,1)} async-done(((bf16[8,16,3840]{2,1,0:T(8,128)(2,1)}), bf16[8,256,3840]{2,1,0:T(8,128)(2,1)}) %all-gather.2.cloned.1.call-update) | async-done | bytes 15728656 | tf_op jit(solution)/shard_map/all_gather | solution.py:96
  161.3 21.5 %bitcast_convert_fusion = bf16[1024,3840]{1,0:T(8,128)(2,1)} fusion(bf16[8,256,3840]{2,1,0:T(8,128)(2,1)} %all-gather.2.cloned.1.call-done, bf16[512,8,256]{2,0,1:T(8,128)(2,1)} %copy.52, bf16[512,8,256]{2,0,1:T(8,128)(2,1)S(1)} %copy-done.5), kind=kOutput, calls=%fused_computation.12 | convolution fusion | flops 16118448128 | bytes 27787264 | tf_op jit(solution)/shard_map/thn,hnd->td/dot_general | solution.py:93
  182.8 183.3 %reduce-scatter.2.cloned.1.call-done = bf16[512,3840]{1,0:T(8,128)(2,1)} async-done(((bf16[1024,3840]{1,0:T(8,128)(2,1)}), bf16[512,3840]{1,0:T(8,128)(2,1)}) %reduce-scatter.2.cloned.1.call-update) | async-done | bytes 3932176 | tf_op jit(solution)/shard_map/reduce_scatter | solution.py:99
  366.1 3.1 fusion.10
  369.4 3.3 fusion.12
  (34 shorter events, 0.9 us)
Async XLA Ops:
  6.5 14.5 %copy-start.2 = (bf16[1024,1024]{1,0:T(8,128)(2,1)S(1)}, bf16[1024,1024]{1,0:T(8,128)(2,1)}, u32[]{:S(2)}) copy-start(bf16[1024,1024]{1,0:T(8,128)(2,1)} %param.7) | copy-start | bytes 6291460
  6.5 154.8 %all-gather.2.cloned.1.call-start = ((), (), s32[]{:S(2)}) async-start(), calls=%async_computation.1 | async-start | bytes 16711680 | tf_op jit(solution)/shard_map/all_gather | solution.py:96
  7.3 358.9 %reduce-scatter.2.cloned.1.call-start = ((), (), s32[]{:S(2)}) async-start(), calls=%async_computation.2 | async-start | bytes 11796480 | tf_op jit(solution)/shard_map/reduce_scatter | solution.py:99
  11.3 12.6 %copy-start.8 = (s32[16]{0:T(128)S(1)}, s32[16]{0:T(128)}, u32[]{:S(2)}) copy-start(s32[16]{0:T(128)} %param.11) | copy-start | bytes 196
  11.3 52.7 %collective-permute-start.1 = (bf16[1024,1024]{0,1:T(8,128)(2,1)}, bf16[1024,1024]{0,1:T(8,128)(2,1)}, u32[]{:S(2)}, u32[]{:S(2)}) collective-permute-start(bf16[1024,1024]{0,1:T(8,128)(2,1)} %copy.36), channel_id=1, source_target_pairs={{0,2},{2,4},{4,6},{6,8},{8,10},{10,12},{12,14},{14,16},{16,18},{18... | collective-permute-start | bytes 6291464 | tf_op jit(solution)/shard_map/ppermute | solution.py:13
  15.1 38.3 %collective-permute-start = (bf16[1024,1024]{1,0:T(8,128)(2,1)}, bf16[1024,1024]{1,0:T(8,128)(2,1)}, u32[]{:S(2)}, u32[]{:S(2)}) collective-permute-start(bf16[1024,1024]{1,0:T(8,128)(2,1)} %param.8), channel_id=1, source_target_pairs={{0,2},{2,4},{4,6},{6,8},{8,10},{10,12},{12,14},{14,16},{16,18},{18... | collective-permute-start | bytes 6291464 | tf_op jit(solution)/shard_map/ppermute | solution.py:13
  38.9 6.4 %copy-start.1 = (bf16[1024,4,256]{2,1,0:T(4,128)(2,1)S(1)}, bf16[1024,4,256]{2,1,0:T(4,128)(2,1)}, u32[]{:S(2)}) copy-start(bf16[1024,4,256]{2,1,0:T(4,128)(2,1)} %reshape.281) | copy-start | bytes 6291460
  53.4 2.2 copy-start.4
  63.9 4.7 %copy-start.6 = (pred[512,1536]{0,1:T(8,128)(4,1)S(1)}, pred[512,1536]{0,1:T(8,128)(4,1)}, u32[]{:S(2)}) copy-start(pred[512,1536]{0,1:T(8,128)(4,1)} %fusion.17) | copy-start | bytes 2359300
  112.1 16.7 %copy-start.3 = (bf16[1536,1024]{0,1:T(8,128)(2,1)S(1)}, bf16[1536,1024]{0,1:T(8,128)(2,1)}, u32[]{:S(2)}) copy-start(bf16[1536,1024]{0,1:T(8,128)(2,1)} %copy.44) | copy-start | bytes 9437188
  141.9 19.4 %copy-start.5 = (bf16[512,8,256]{2,0,1:T(8,128)(2,1)S(1)}, bf16[512,8,256]{2,0,1:T(8,128)(2,1)}, u32[]{:S(2)}) copy-start(bf16[512,8,256]{2,0,1:T(8,128)(2,1)} %copy.51) | copy-start | bytes 6291460
  182.8 186.4 %copy-start.7 = (f32[3840]{0:T(1024)S(1)}, f32[3840]{0:T(1024)}, u32[]{:S(2)}) copy-start(f32[3840]{0:T(1024)} %param.10) | copy-start | bytes 46084
  366.1 3.3 copy-start
Sparse Core Ops, SparseCore 0:
  9.6 151.6 all-gather.1
  183.0 183.1 reduce-scatter.1
where the time goes:
time: 380 us
  waiting for transfers between devices  199 us (52%)
  matrix products  72.4 us (19%)
  other arithmetic  43.5 us (11%)
  local copies, waits for them, and re-layouts  42.4 us (11%)
  between operations  13.5 us (4%)
  starting transfers between devices  8.37 us (2%)
    reduce_scatter x1, waiting for transfers between devices, on_device(): lax.psum_scatter(partial_value.astype(jnp.bfloat16), 'tp', scatter_dimens...  183 us
    sub x2, other arithmetic, on_device(): expo = jnp.exp(scores - top)  31.5 us
    dot_general x2, matrix products, on_device(): jnp.einsum('hgqk,khd->qhgd', weights, value_block, preferred_element_type...  27.2 us
    dot_general x4, matrix products, score_part(): jnp.einsum('qhgd,khd->hgqk', query_block, key_block, preferred_element_ty...  23.7 us
    dot_general x1, matrix products, on_device(): jnp.einsum('thn,hnd->td', attn, lax.all_gather(w_out, 'ctx', axis=1, tile...  21.5 us
    all_gather x1, waiting for transfers between devices, on_device(): lax.all_gather(w_out, 'ctx', axis=1, tiled=True)  15.4 us
    slice x3, local copies, waits for them, and re-layouts, on_device(): all_vals[lower:lower + key_block_size]  12.8 us
    unnamed x22, local copies, waits for them, and re-layouts  11.8 us
  transfers between devices with their start and end apart: 4, of which 2 were waited for; matrix products, arithmetic and copies ran while one was open for 34% of the time, Pallas kernels for 0%

commit v1 on v0

--- a/solution.py
+++ b/solution.py
@@ -5,6 +5,18 @@
 
 HEAD_SIZE = 256
 ATTEND_WINDOW = 1024
+
+
+def gather_by_bits(x, axis, dim):
+    ways, here = (lax.axis_size(axis), lax.axis_index(axis))
+    grown, reach = (x, 1)
+    while reach < ways:
+        theirs = lax.ppermute(grown, axis, [(d, d ^ reach) for d in range(ways)])
+        mine_first = jnp.concatenate([grown, theirs], axis=dim)
+        theirs_first = jnp.concatenate([theirs, grown], axis=dim)
+        grown = jnp.where(here & reach == 0, mine_first, theirs_first)
+        reach = 2 * reach
+    return grown
 
 
 def shifted(shard, axis, by):
@@ -91,10 +103,7 @@
         )
     attn = jnp.concatenate(outputs, axis=0).reshape(tok_local, heads_local, HEAD_SIZE)
     partial_value = jnp.einsum(
-        "thn,hnd->td",
-        attn,
-        lax.all_gather(w_out, "ctx", axis=1, tiled=True),
-        preferred_element_type=jnp.float32,
+        "thn,hnd->td", attn, gather_by_bits(w_out, "ctx", 1), preferred_element_type=jnp.float32
     )
     mine = lax.psum_scatter(
         partial_value.astype(jnp.bfloat16), "tp", scatter_dimension=0, tiled=True

time: 380 us -> 678 us (1.78)
  waiting for transfers between devices: 199 us -> 453 us
  starting transfers between devices: 8.37 us -> 37.4 us
  other arithmetic: 43.5 us -> 57.4 us
    ppermute x0 -> x4, waiting for transfers between devices: none -> 358 us  [gather_by_bits(): theirs = lax.ppermute(grown, axis, [(d, d ^ reach) for d in range(ways)])]
    reduce_scatter x1, waiting for transfers between devices: 183 us -> 94.9 us  [on_device(): lax.psum_scatter(partial_value.astype(jnp.bfloat16), 'tp', scatter_dimens...]
    ppermute x0 -> x4, starting transfers between devices: none -> 29 us  [gather_by_bits(): theirs = lax.ppermute(grown, axis, [(d, d ^ reach) for d in range(ways)])]
    all_gather x1 -> x0, waiting for transfers between devices: 15.4 us -> none  [on_device(): lax.all_gather(w_out, 'ctx', axis=1, tiled=True)]
    select_n x0 -> x3, other arithmetic: none -> 15.3 us  [gather_by_bits(): grown = jnp.where(here & reach == 0, mine_first, theirs_first)]
    unnamed x22 -> x26, local copies, waits for them, and re-layouts: 11.8 us -> 13.9 us
  transfers between devices with their start and end apart: 4 -> 7, of which waited for: 2 -> 4; matrix products, arithmetic and copies ran while one was open for 34% -> 19% of each run, Pallas kernels for 0% -> 0%
where the time goes in v1:
time: 678 us; the launch traced here: 677 us
  waiting for transfers between devices  453 us (67%)
  matrix products  71.4 us (11%)
  other arithmetic  57.4 us (8%)
  local copies, waits for them, and re-layouts  44.4 us (7%)
  starting transfers between devices  37.4 us (6%)
  between operations  13.6 us (2%)
    ppermute x4, waiting for transfers between devices, gather_by_bits(): theirs = lax.ppermute(grown, axis, [(d, d ^ reach) for d in range(ways)])  358 us
    reduce_scatter x1, waiting for transfers between devices, on_device(): lax.psum_scatter(partial_value.astype(jnp.bfloat16), 'tp', scatter_dimens...  94.9 us
    sub x2, other arithmetic, on_device(): expo = jnp.exp(scores - top)  31 us
    ppermute x4, starting transfers between devices, gather_by_bits(): theirs = lax.ppermute(grown, axis, [(d, d ^ reach) for d in range(ways)])  29 us
    dot_general x2, matrix products, on_device(): jnp.einsum('hgqk,khd->qhgd', weights, value_block, preferred_element_type...  26.8 us
    dot_general x1, matrix products, on_device(): jnp.einsum('thn,hnd->td', attn, gather_by_bits(w_out, 'ctx', 1), preferre...  23.3 us
    dot_general x4, matrix products, score_part(): jnp.einsum('qhgd,khd->hgqk', query_block, key_block, preferred_element_ty...  21.4 us
    select_n x3, other arithmetic, gather_by_bits(): grown = jnp.where(here & reach == 0, mine_first, theirs_first)  15.3 us
  transfers between devices with their start and end apart: 7, of which 4 were waited for; matrix products, arithmetic and copies ran while one was open for 19% of the time, Pallas kernels for 0%

profile of v1, /device:TPU:0, one launch (start us, length us, event | category | flops | bytes accessed | tf_op | source)
XLA Modules:
  0.0 677.1 jit_solution(4178885970770630075)
XLA Ops:
  6.5 4.1 copy.36
  10.6 3.8 collective-permute-start.1
  14.5 4.5 collective-permute-start
  20.3 2.8 reshape.281
  23.3 4.0 fusion.33
  27.3 2.5 copy.73
  29.8 2.9 copy.74
  32.9 2.7 maximum_select_fusion.10
  37.7 4.6 multiply_bitcast_fusion.3
  42.3 2.6 fusion.26
  44.9 36.0 %collective-permute-done.3 = bf16[8,32,3840]{2,1,0:T(8,128)(2,1)S(1)} collective-permute-done((bf16[8,32,3840]{2,1,0:T(8,128)(2,1)S(1)}, bf16[8,32,3840]{2,1,0:T(8,128)(2,1)S(1)}, u32[]{:S(2)}, u32[]{:S(2)}) %collective-permute-start.3) | collective-permute-done | bytes 1966112 | tf_op jit(solution)/shard_map/ppermute | solution.py:14
  83.3 25.9 %collective-permute-start.4 = (bf16[8,64,3840]{2,1,0:T(8,128)(2,1)}, bf16[8,64,3840]{2,1,0:T(8,128)(2,1)}, u32[]{:S(2)}, u32[]{:S(2)}) collective-permute-start(bf16[8,64,3840]{2,1,0:T(8,128)(2,1)} %maximum_select_fusion.9), channel_id=1, source_target_pairs={{0,8},{2,10},{4,12},{6,14},{8,0},{10,2},{12,4},{14,6},{16,24},{18,... | collective-permute-start | bytes 11796488 | tf_op jit(solution)/shard_map/ppermute | solution.py:14
  109.2 8.2 %multiply_bitcast_fusion = f32[4,2,512,1024]{2,3,1,0:T(8,128)} fusion(bf16[512,4,2,256]{0,3,2,1:T(8,128)(2,1)S(1)} %bitcast.54, bf16[1024,4,256,1]{2,1,0,3:T(4,128)(2,1)S(1)} %bitcast.58), kind=kOutput, calls=%fused_computation.10 | convolution fusion | flops 2151677952 | bytes 20971520 | tf_op jit(solution)/shard_map/qhgd,khd->hgqk/dot_general | solution.py:36
  121.9 4.0 multiply_bitcast_fusion.1
  125.9 14.3 %fusion.40 = (f32[4,2,512]{2,1,0:T(2,128)S(1)}, f32[4,2,512,1536]{2,3,1,0:T(8,128)}) fusion(f32[4,2,512,512]{2,3,1,0:T(8,128)} %multiply_bitcast_fusion.3, f32[4,2,512,1024]{2,3,1,0:T(8,128)S(1)} %multiply_bitcast_fusion.1, pred[512,1536]{0,1:T(8,128)(4,1)S(1)} %fusion.24), kind=kOutput, calls=%fused_computation.68 | output fusion | flops 25167360 | bytes 51134464 | tf_op jit(solution)/shard_map/sub | solution.py:96
  140.2 54.5 %collective-permute-done.4 = bf16[8,64,3840]{2,1,0:T(8,128)(2,1)} collective-permute-done((bf16[8,64,3840]{2,1,0:T(8,128)(2,1)}, bf16[8,64,3840]{2,1,0:T(8,128)(2,1)}, u32[]{:S(2)}, u32[]{:S(2)}) %collective-permute-start.4) | collective-permute-done | bytes 3932192 | tf_op jit(solution)/shard_map/ppermute | solution.py:14
  194.7 10.3 %maximum_select_fusion.6 = bf16[8,128,3840]{2,1,0:T(8,128)(2,1)} fusion(bf16[8,64,3840]{2,1,0:T(8,128)(2,1)} %collective-permute-done.4, bf16[8,64,3840]{2,1,0:T(8,128)(2,1)} %maximum_select_fusion.9, pred[]{:T(512)S(6)} %eq.53), kind=kLoop, calls=%fused_computation.34 | loop fusion | flops 35389440 | bytes 15728641 | tf_op jit(solution)/shard_map/jit(_where)/select_n | solution.py:17
  205.0 2.8 collective-permute-start.5
  207.7 3.6 fusion.34
  211.3 4.7 copy.34
  216.0 13.9 %fusion.29 = bf16[4,256,2,512]{3,1,2,0:T(8,128)(2,1)} fusion(bf16[1536,4,256,1]{0,2,3,1:T(8,128)(2,1)} %bitcast.62, f32[4,2,512,1536]{2,3,1,0:T(8,128)} %get-tuple-element.22, f32[4,2,512]{2,1,0:T(2,128)S(1)} %get-tuple-element.21), kind=kOutput, calls=%fused_computation.48 | convolution fusion | flops 3234856960 | bytes 30425088 | tf_op jit(solution)/shard_map/hgqk,khd->qhgd/dot_general | solution.py:98
  229.9 3.9 copy.51
  233.8 4.6 copy.44
  239.7 4.5 multiply_bitcast_fusion.2
  244.3 16.7 %fusion.39 = (f32[4,2,512]{2,1,0:T(2,128)S(1)}, f32[4,2,512,1536]{2,3,1,0:T(8,128)}) fusion(f32[4,2,512,1024]{2,3,1,0:T(8,128)} %multiply_bitcast_fusion, f32[4,2,512,512]{2,3,1,0:T(8,128)} %multiply_bitcast_fusion.2, pred[512,1536]{0,1:T(8,128)(4,1)} %fusion.26), kind=kOutput, calls=%fused_computation.67 | output fusion | flops 25167360 | bytes 51134464 | tf_op jit(solution)/shard_map/sub | solution.py:96
  261.0 12.9 %fusion.28 = bf16[4,256,2,512]{3,1,2,0:T(8,128)(2,1)} fusion(bf16[1536,4,256,1]{0,2,3,1:T(8,128)(2,1)S(1)} %bitcast.61, f32[4,2,512,1536]{2,3,1,0:T(8,128)} %get-tuple-element.20, f32[4,2,512]{2,1,0:T(2,128)S(1)} %get-tuple-element.19), kind=kOutput, calls=%fused_computation.47 | convolution fusion | flops 3234856960 | bytes 30425088 | tf_op jit(solution)/shard_map/hgqk,khd->qhgd/dot_general | solution.py:98
  273.9 4.1 copy.52
  278.0 267.4 %collective-permute-done.5 = bf16[8,128,3840]{2,1,0:T(8,128)(2,1)} collective-permute-done((bf16[8,128,3840]{2,1,0:T(8,128)(2,1)}, bf16[8,128,3840]{2,1,0:T(8,128)(2,1)}, u32[]{:S(2)}, u32[]{:S(2)}) %collective-permute-start.5) | collective-permute-done | bytes 7864352 | tf_op jit(solution)/shard_map/ppermute | solution.py:14
  545.4 23.3 %bitcast_convert_fusion = bf16[1024,3840]{1,0:T(8,128)(2,1)} fusion(bf16[8,128,3840]{2,1,0:T(8,128)(2,1)} %collective-permute-done.5, bf16[8,128,3840]{2,1,0:T(8,128)(2,1)} %maximum_select_fusion.6, pred[]{:T(512)S(6)} %eq.52, bf16[512,8,256]{2,0,1:T(8,128)(2,1)} %copy.52, bf16[512,8,256]{2,0,1:T(8,128)(2,1)S(1)} %copy-done.8), kind=kOutput, calls=%fused_computation.19 | convolution fusion | flops 16189227008 | bytes 27787264 | tf_op jit(solution)/shard_map/thn,hnd->td/dot_general | solution.py:105
  568.7 94.9 %reduce-scatter.2.cloned.1.call-done = bf16[512,3840]{1,0:T(8,128)(2,1)} async-done(((bf16[1024,3840]{1,0:T(8,128)(2,1)}), bf16[512,3840]{1,0:T(8,128)(2,1)}) %reduce-scatter.2.cloned.1.call-update) | async-done | bytes 3932176 | tf_op jit(solution)/shard_map/reduce_scatter | solution.py:108
  663.6 3.1 fusion.17
  666.9 3.3 fusion.19
  (46 shorter events, 12.1 us)
Async XLA Ops:
  6.5 13.8 %copy-start.5 = (bf16[1024,1024]{1,0:T(8,128)(2,1)S(1)}, bf16[1024,1024]{1,0:T(8,128)(2,1)}, u32[]{:S(2)}) copy-start(bf16[1024,1024]{1,0:T(8,128)(2,1)} %param.7) | copy-start | bytes 6291460
  6.5 657.1 %reduce-scatter.2.cloned.1.call-start = ((), (), s32[]{:S(2)}) async-start(), calls=%async_computation.1 | async-start | bytes 11796480 | tf_op jit(solution)/shard_map/reduce_scatter | solution.py:108
  10.6 12.5 %copy-start.10 = (s32[16]{0:T(128)S(1)}, s32[16]{0:T(128)}, u32[]{:S(2)}) copy-start(s32[16]{0:T(128)} %param.11) | copy-start | bytes 196
  10.6 109.2 %collective-permute-start.1 = (bf16[1024,1024]{0,1:T(8,128)(2,1)}, bf16[1024,1024]{0,1:T(8,128)(2,1)}, u32[]{:S(2)}, u32[]{:S(2)}) collective-permute-start(bf16[1024,1024]{0,1:T(8,128)(2,1)} %copy.36), channel_id=1, source_target_pairs={{0,2},{2,4},{4,6},{6,8},{8,10},{10,12},{12,14},{14,16},{16,18},{18... | collective-permute-start | bytes 6291464 | tf_op jit(solution)/shard_map/ppermute | solution.py:25
  14.5 103.0 %collective-permute-start = (bf16[1024,1024]{1,0:T(8,128)(2,1)}, bf16[1024,1024]{1,0:T(8,128)(2,1)}, u32[]{:S(2)}, u32[]{:S(2)}) collective-permute-start(bf16[1024,1024]{1,0:T(8,128)(2,1)} %param.8), channel_id=1, source_target_pairs={{0,2},{2,4},{4,6},{6,8},{8,10},{10,12},{12,14},{14,16},{16,18},{18... | collective-permute-start | bytes 6291464 | tf_op jit(solution)/shard_map/ppermute | solution.py:25
  19.0 13.9 %collective-permute-start.2 = (bf16[8,16,3840]{2,1,0:T(8,128)(2,1)}, bf16[8,16,3840]{2,1,0:T(8,128)(2,1)}, u32[]{:S(2)}, u32[]{:S(2)}) collective-permute-start(bf16[8,16,3840]{2,1,0:T(8,128)(2,1)} %param.9), channel_id=1, source_target_pairs={{0,2},{2,0},{4,6},{6,4},{8,10},{10,8},{12,14},{14,12},{16,18},{18,... | collective-permute-start | bytes 2949128 | tf_op jit(solution)/shard_map/ppermute | solution.py:14
  32.7 5.0 copy-start
  35.6 45.3 %collective-permute-start.3 = (bf16[8,32,3840]{2,1,0:T(8,128)(2,1)S(1)}, bf16[8,32,3840]{2,1,0:T(8,128)(2,1)S(1)}, u32[]{:S(2)}, u32[]{:S(2)}) collective-permute-start(bf16[8,32,3840]{2,1,0:T(8,128)(2,1)S(1)} %maximum_select_fusion.10), channel_id=1, source_target_pairs={{0,4},{2,6},{4,0},{6,2},{8,12},{10,14},{12,8},{14,10},{16,20},{18,... | collective-permute-start | bytes 5898248 | tf_op jit(solution)/shard_map/ppermute | solution.py:14
  42.3 66.9 %copy-start.4 = (bf16[1024,4,256]{2,1,0:T(4,128)(2,1)S(1)}, bf16[1024,4,256]{2,1,0:T(4,128)(2,1)}, u32[]{:S(2)}) copy-start(bf16[1024,4,256]{2,1,0:T(4,128)(2,1)} %reshape.281) | copy-start | bytes 6291460
  83.3 111.4 %collective-permute-start.4 = (bf16[8,64,3840]{2,1,0:T(8,128)(2,1)}, bf16[8,64,3840]{2,1,0:T(8,128)(2,1)}, u32[]{:S(2)}, u32[]{:S(2)}) collective-permute-start(bf16[8,64,3840]{2,1,0:T(8,128)(2,1)} %maximum_select_fusion.9), channel_id=1, source_target_pairs={{0,8},{2,10},{4,12},{6,14},{8,0},{10,2},{12,4},{14,6},{16,24},{18,... | collective-permute-start | bytes 11796488 | tf_op jit(solution)/shard_map/ppermute | solution.py:14
  117.4 2.2 copy-start.7
  119.8 2.1 copy-start.1
  140.2 67.6 %copy-start.2 = (bf16[2048,1024]{1,0:T(8,128)(2,1)S(1)}, bf16[2048,1024]{1,0:T(8,128)(2,1)}, u32[]{:S(2)}) copy-start(bf16[2048,1024]{1,0:T(8,128)(2,1)} %copy-done.1) | copy-start | bytes 12582916
  205.0 340.4 %collective-permute-start.5 = (bf16[8,128,3840]{2,1,0:T(8,128)(2,1)}, bf16[8,128,3840]{2,1,0:T(8,128)(2,1)}, u32[]{:S(2)}, u32[]{:S(2)}) collective-permute-start(bf16[8,128,3840]{2,1,0:T(8,128)(2,1)} %maximum_select_fusion.6), channel_id=1, source_target_pairs={{0,16},{2,18},{4,20},{6,22},{8,24},{10,26},{12,28},{14,30},{16,0},... | collective-permute-start | bytes 23592968 | tf_op jit(solution)/shard_map/ppermute | solution.py:14
  244.3 16.7 %copy-start.6 = (bf16[1536,1024]{0,1:T(8,128)(2,1)S(1)}, bf16[1536,1024]{0,1:T(8,128)(2,1)}, u32[]{:S(2)}) copy-start(bf16[1536,1024]{0,1:T(8,128)(2,1)} %copy.44) | copy-start | bytes 9437188
  273.9 271.5 %copy-start.8 = (bf16[512,8,256]{2,0,1:T(8,128)(2,1)S(1)}, bf16[512,8,256]{2,0,1:T(8,128)(2,1)}, u32[]{:S(2)}) copy-start(bf16[512,8,256]{2,0,1:T(8,128)(2,1)} %copy.51) | copy-start | bytes 6291460
  568.7 98.0 %copy-start.9 = (f32[3840]{0:T(1024)S(1)}, f32[3840]{0:T(1024)}, u32[]{:S(2)}) copy-start(f32[3840]{0:T(1024)} %param.10) | copy-start | bytes 46084
  663.6 3.3 copy-start.3
Sparse Core Ops, SparseCore 0:
  568.9 94.7 reduce-scatter.1
